TPU v7x, 256 devices: a whole 4x4x8 slice. The times are simulated.
256 devices in a mesh: freq: 16 (over z, core), tile: 16 (over y, x).
Axes of the slice: x: 4, y: 4, z: 8, core: 2. Of those that a mesh axis runs over, the one named last changes fastest.
Arguments:
- focal_field: bfloat16 [16, 16384, 2, 256], P('freq', 'tile'), may hold values from -6 to 6
- v_factors: bfloat16 [16, 16, 16384, 128], P('freq', None, 'tile'), may hold values from -0.1875 to 0.1875
- u_factors: bfloat16 [16, 16384, 16, 128], P('freq', 'tile'), may hold values from -0.125 to 0.125
- ranks: int32 [16, 16, 16], P('freq', None, 'tile'), may hold values from 16 to 64, as said below
- tile_mask: int32 [16, 16, 16], P('freq', None, 'tile'), may hold values 0 or 1
- initial_focus: bfloat16 [16, 32, 1024, 256], P('tile', None, 'freq'), may hold values from -6 to 6
- mute_starts: int32 [16, 1024, 256], P('tile', 'freq'), may hold values from 1 to 31
- taper: float32 [16, 1024], P('tile', 'freq'), may hold values from 0.3 to 3
Outputs:
- focusing: bfloat16 [16, 32, 1024, 256], P('tile', None, 'freq')
- correlation: float32 [16, 256, 256], P('freq', 'tile')
Inputs may be any that keep to these rules, and one draw needn't show every extreme that they name: `ranks`: in every frequency some tile has rank exactly 64; no rank is below 16.
All inputs are finite; a program needn't handle non-finite values. No bound on the sum of `tile_mask` on one device may be relied on, other than what follows from the above.
Results may differ from a plain program's by a relative error of at most 0.009.
Values may be sent and summed in bfloat16 or wider, within the bound.
No kernel may reach another device: no remote copies, remote signals or barrier semaphores. Data moves between devices by JAX's collectives and lax.ppermute only.
A program may use at most 64 MiB of HBM per device.

v0:
```python
import math
import jax
import jax.numpy as jnp
from jax import lax
from jax.sharding import PartitionSpec as P


def dft_table(trace_length, freq_count):
    clock_moments = jnp.arange(trace_length, dtype=jnp.float32)
    angular_rate = jnp.arange(freq_count, dtype=jnp.float32) + 1.0
    rotation_radians = 2.0 * math.pi / trace_length * clock_moments[:, None] * angular_rate[None, :]
    return jnp.stack([jnp.cos(rotation_radians), -jnp.sin(rotation_radians)], axis=2) / jnp.sqrt(
        jnp.float32(freq_count)
    )


def stacked_rhs(received):
    sources = received.shape[0]
    columns = received.shape[3]
    real_c = received[:, :, 0, :]
    imag_c = received[:, :, 1, :]
    upper = jnp.concatenate([real_c, -imag_c], axis=1)
    lower = jnp.concatenate([imag_c, real_c], axis=1)
    return jnp.concatenate([upper, lower], axis=2).reshape(sources * upper.shape[1], 2 * columns)


def body(focal_field, v_factors, u_factors, ranks, tile_mask, initial_focus, mute_starts, taper):
    tile_count = lax.axis_size("tile")
    rank_max = v_factors.shape[3] // 2
    focal_count = focal_field.shape[3]
    tile_rows = focal_field.shape[1]
    flat_field = focal_field[0].reshape(tile_rows, 2 * focal_count)
    moments = jnp.einsum(
        "irk,rc->ikc", v_factors[0], flat_field, preferred_element_type=jnp.float32
    )
    real_part = moments[:, :rank_max, :focal_count] - moments[:, rank_max:, focal_count:]
    imag_part = moments[:, :rank_max, focal_count:] + moments[:, rank_max:, :focal_count]
    levels = jnp.arange(rank_max, dtype=jnp.int32)
    retained = (
        (levels[None, :] < ranks[0, :, 0][:, None]) & (tile_mask[0, :, 0][:, None] > 0)
    ).astype(jnp.float32)
    coeffs = jnp.stack(
        [real_part * retained[:, :, None], imag_part * retained[:, :, None]], axis=2
    ).astype(jnp.bfloat16)
    u_rows = u_factors[0]
    received = lax.all_to_all(coeffs, "tile", split_axis=0, concat_axis=0, tiled=True)
    columns = received.shape[3]
    product = jnp.dot(
        u_rows.reshape(tile_rows, -1), stacked_rhs(received), preferred_element_type=jnp.float32
    )
    fields = product.reshape(tile_rows, 2, columns).astype(jnp.bfloat16)
    trace_length = initial_focus.shape[1]
    gathered = lax.all_to_all(fields[None], "freq", split_axis=1, concat_axis=0, tiled=True)
    dft_weights = dft_table(trace_length, gathered.shape[0])
    trace_signal = jnp.einsum(
        "tfc,fscn->tsn", dft_weights, gathered.astype(jnp.float32), precision=lax.Precision.HIGHEST
    )
    group_rows = trace_signal.shape[1]
    clock_moments = jnp.arange(trace_length, dtype=jnp.int32)
    silenced_wavefield = jnp.where(
        clock_moments[:, None, None] < mute_starts[0][None, :, :], trace_signal, 0.0
    )
    focusing = (initial_focus[0].astype(jnp.float32) - silenced_wavefield).astype(jnp.bfloat16)
    weighted = (focusing.astype(jnp.float32) * taper[0][None, :, None]).astype(jnp.bfloat16)
    flat_focus = focusing.reshape(trace_length * group_rows, focal_count)
    flat_weighted = weighted.reshape(trace_length * group_rows, focal_count)
    partial_value = lax.dot_general(
        flat_focus, flat_weighted, (((0,), (0,)), ((), ())), preferred_element_type=jnp.float32
    )
    normalizer = 1.0 / float(tile_count * trace_length * group_rows)
    summed_total = lax.psum(partial_value.astype(jnp.bfloat16), "tile").astype(jnp.float32)
    share_rows = focal_count // tile_count
    own_rows = lax.dynamic_slice_in_dim(
        summed_total, lax.axis_index("tile") * share_rows, share_rows, 0
    )
    return (focusing[None], (own_rows * normalizer)[None])


def solution(mesh):
    placed = (
        P("freq", "tile", None, None),
        P("freq", None, "tile", None),
        P("freq", "tile", None, None),
        P("freq", None, "tile"),
        P("freq", None, "tile"),
        P("tile", None, "freq", None),
        P("tile", "freq", None),
        P("tile", "freq"),
    )
    return jax.shard_map(
        body,
        mesh=mesh,
        in_specs=placed,
        out_specs=(P("tile", None, "freq", None), P("freq", "tile", None)),
        check_vma=False,
    )
```

profile of v0, /device:TPU:2, one launch (start us, length us, event | category | flops | bytes accessed | tf_op | source)
XLA Modules:
  0.0 179.9 jit_solution(2746314441526483126)
XLA Ops:
  7.2 0.0 copy-start.5
  7.2 1.7 reshape.179
  8.9 0.0 copy-done.5
  8.9 0.0 copy-start.1
  9.0 4.6 %fusion.3 = f32[16,128,512]{2,1,0:T(8,128)S(1)} fusion(bf16[1024,512,1]{1,0,2:T(8,128)(2,1)S(1)} %reshape.179, bf16[1,16,1024,128]{3,2,1,0:T(8,128)(2,1)} %param.9), kind=kOutput, calls=%fused_computation.3 | convolution fusion | flops 2147483648 | bytes 9437184 | tf_op jit(solution)/shard_map/irk,rc->ikc/dot_general | solution.py:33
  13.5 0.0 copy-done.1
  13.6 0.1 fusion.27
  13.6 0.4 fusion.18
  14.0 0.1 pad_maximum_fusion
  14.1 0.1 copy.24
  14.2 23.1 %all_to_all.17 = bf16[16,64,2,256]{3,1,2,0:T(8,128)(2,1)S(1)} all-to-all(bf16[16,64,2,256]{3,1,2,0:T(8,128)(2,1)S(1)} %copy.24), channel_id=1, replica_groups=mesh['freq'=16,'tile'=16] {'tile'}, dimensions={0} | all-to-all | bytes 2097152 | tf_op jit(solution)/shard_map/all_to_all | solution.py:46
  37.3 0.1 slice_bitcast_fusion
  37.4 0.0 copy-start.2
  37.4 0.2 maximum_maximum_fusion
  37.6 1.9 %copy-done.2 = bf16[1,1024,16,128]{3,2,1,0:T(8,128)(2,1)S(1)} copy-done((bf16[1,1024,16,128]{3,2,1,0:T(8,128)(2,1)S(1)}, bf16[1,1024,16,128]{3,2,1,0:T(8,128)(2,1)}, u32[]{:S(2)}) %copy-start.2) | copy-done | bytes 4194328
  39.6 2.4 %fusion.7 = bf16[512,1024]{1,0:T(8,128)(2,1)S(1)} fusion(bf16[2048,512]{1,0:T(8,128)(2,1)S(1)} %bitcast.54, bf16[128,8,16,128]{3,2,1,0:T(8,128)(2,1)S(1)} %bitcast.59), kind=kOutput, calls=%fused_computation.12 | convolution fusion | flops 2148007936 | bytes 7340032 | tf_op jit(solution)/shard_map/dot_general | solution.py:48
  42.0 0.0 copy-start.3
  42.0 0.0 copy-start.4
  42.0 2.0 %copy.26 = bf16[1,1024,2,256]{3,2,0,1:T(2,128)(2,1)} copy(bf16[1,1024,2,256]{1,3,2,0:T(8,128)(2,1)S(1)} %bitcast.56) | data formatting | bytes 2097152 | tf_op jit(solution)/shard_map/convert_element_type | solution.py:51
  44.0 8.6 %all-to-all-start.1 = ((bf16[1,1024,2,256]{3,2,0,1:T(2,128)(2,1)}), bf16[1,1024,2,256]{3,2,0,1:T(2,128)(2,1)S(1)}, u32[]{:S(2)}, u32[]{:S(2)}) async-start(bf16[1,1024,2,256]{3,2,0,1:T(2,128)(2,1)} %copy.26), calls=%async_computation.1 | async-start | bytes 2097152 | tf_op jit(solution)/shard_map/all_to_all | solution.py:53
  52.6 0.0 copy-start
  52.6 0.0 all-reduce.2.cloned.1.call-start
  52.7 0.1 multiply_cosine_fusion
  52.8 26.3 %all-to-all-done.1 = bf16[1,1024,2,256]{3,2,0,1:T(2,128)(2,1)S(1)} async-done(((bf16[1,1024,2,256]{3,2,0,1:T(2,128)(2,1)}), bf16[1,1024,2,256]{3,2,0,1:T(2,128)(2,1)S(1)}, u32[]{:S(2)}, u32[]{:S(2)}) %all-to-all-start.1) | async-done | bytes 1048608 | tf_op jit(solution)/shard_map/all_to_all | solution.py:53
  79.1 0.0 copy-done.3
  79.1 0.0 copy-done.4
  79.1 1.9 %fusion.5 = bf16[32,64,256]{2,0,1:T(8,128)(2,1)S(1)} fusion(bf16[16,64,2,256]{3,2,1,0:T(2,128)(2,1)S(1)} %bitcast.55, bf16[1,32,64,256]{3,2,1,0:T(8,128)(2,1)S(1)} %copy-done.3, s32[64,256]{1,0:T(8,128)S(1)} %bitcast.60, f32[32,16,1]{0,1,2:T(8,128)S(1)} %get-tuple-element.13, f32[32,16,1]{0,1,2:T(8,128)S(1)} %get-tuple-element.12), kind=kOutput, calls=%fused_computation.7 | convolution fusion | flops 203950080 | bytes 3215360 | tf_op jit(solution)/shard_map/tfc,fscn->tsn/dot_general | solution.py:55
  81.1 1.3 fusion.11
  82.4 0.0 all-reduce.2.cloned.1.call-update
  82.4 1.6 copy.29
  83.9 87.8 %all-reduce.2.cloned.1.call-done = bf16[256,256]{1,0:T(8,128)(2,1)} async-done(((bf16[256,256]{1,0:T(8,128)(2,1)}), bf16[256,256]{1,0:T(8,128)(2,1)}) %all-reduce.2.cloned.1.call-update) | async-done | bytes 131088 | tf_op jit(solution)/shard_map/psum | solution.py:71
  171.7 1.3 multiply_bitcast_fusion
  (5 shorter events, 0.1 us)
Async XLA Ops:
  7.2 1.8 copy-start.5
  8.9 4.6 %copy-start.1 = (s32[1,16,1]{1,2,0:T(1,128)S(1)}, s32[1,16,1]{1,2,0:T(1,128)}, u32[]{:S(2)}) copy-start(s32[1,16,1]{1,2,0:T(1,128)} %param.11) | copy-start | bytes 196
  37.4 2.2 %copy-start.2 = (bf16[1,1024,16,128]{3,2,1,0:T(8,128)(2,1)S(1)}, bf16[1,1024,16,128]{3,2,1,0:T(8,128)(2,1)}, u32[]{:S(2)}) copy-start(bf16[1,1024,16,128]{3,2,1,0:T(8,128)(2,1)} %param.10) | copy-start | bytes 12582916
  42.0 37.1 %copy-start.3 = (bf16[1,32,64,256]{3,2,1,0:T(8,128)(2,1)S(1)}, bf16[1,32,64,256]{3,2,1,0:T(8,128)(2,1)}, u32[]{:S(2)}) copy-start(bf16[1,32,64,256]{3,2,1,0:T(8,128)(2,1)} %param.13) | copy-start | bytes 3145732
  42.0 37.1 %copy-start.4 = (s32[1,64,256]{2,1,0:T(8,128)S(1)}, s32[1,64,256]{2,1,0:T(8,128)}, u32[]{:S(2)}) copy-start(s32[1,64,256]{2,1,0:T(8,128)} %param.14) | copy-start | bytes 196612
  44.0 35.1 %all-to-all-start.1 = ((bf16[1,1024,2,256]{3,2,0,1:T(2,128)(2,1)}), bf16[1,1024,2,256]{3,2,0,1:T(2,128)(2,1)S(1)}, u32[]{:S(2)}, u32[]{:S(2)}) async-start(bf16[1,1024,2,256]{3,2,0,1:T(2,128)(2,1)} %copy.26), calls=%async_computation.1 | async-start | bytes 2097152 | tf_op jit(solution)/shard_map/all_to_all | solution.py:53
  52.6 28.4 %copy-start = (f32[1,64]{1,0:T(1,128)S(1)}, f32[1,64]{1,0:T(1,128)}, u32[]{:S(2)}) copy-start(f32[1,64]{1,0:T(1,128)} %param.15) | copy-start | bytes 772
  52.6 119.1 %all-reduce.2.cloned.1.call-start = ((), (), s32[]{:S(2)}) async-start(), calls=%async_computation.2 | async-start | bytes 262144 | tf_op jit(solution)/shard_map/psum | solution.py:71
Sparse Core Ops, SparseCore 0:
  82.5 89.1 all-reduce.1
where the time goes:
time: 180 us
  waiting for transfers between devices  114 us (63%)
  blocking collectives  23.1 us (13%)
  between operations  14.2 us (8%)
  matrix products  10.2 us (6%)
  starting transfers between devices  8.61 us (5%)
  local copies, waits for them, and re-layouts  7.51 us (4%)
  other arithmetic  2.2 us (1%)
    psum x1, waiting for transfers between devices, body(): lax.psum(partial_value.astype(jnp.bfloat16), 'tile').astype(jnp.float32)  87.8 us
    all_to_all x1, waiting for transfers between devices, body(): lax.all_to_all(fields[None], 'freq', split_axis=1, concat_axis=0, tiled=T...  26.3 us
    all_to_all x1, blocking collectives, body(): lax.all_to_all(coeffs, 'tile', split_axis=0, concat_axis=0, tiled=True)  23.1 us
    all_to_all x1, starting transfers between devices, body(): lax.all_to_all(fields[None], 'freq', split_axis=1, concat_axis=0, tiled=T...  8.57 us
    dot_general x1, matrix products, body(): jnp.einsum('irk,rc->ikc', v_factors[0], flat_field, preferred_element_typ...  4.58 us
  transfers between devices with their start and end apart: 2, of which 2 were waited for; matrix products, arithmetic and copies ran while one was open for 1% of the time, Pallas kernels for 0%

commit v1 on v0

--- a/solution.py
+++ b/solution.py
@@ -68,7 +68,9 @@
         flat_focus, flat_weighted, (((0,), (0,)), ((), ())), preferred_element_type=jnp.float32
     )
     normalizer = 1.0 / float(tile_count * trace_length * group_rows)
-    summed_total = lax.psum(partial_value.astype(jnp.bfloat16), "tile").astype(jnp.float32)
+    summed_total = jnp.sum(
+        lax.all_gather(partial_value.astype(jnp.bfloat16), "tile"), axis=0
+    ).astype(jnp.float32)
     share_rows = focal_count // tile_count
     own_rows = lax.dynamic_slice_in_dim(
         summed_total, lax.axis_index("tile") * share_rows, share_rows, 0

time: 180 us -> 138 us (0.77)
  waiting for transfers between devices: 114 us -> 70.8 us
    psum x1 -> x0, waiting for transfers between devices: 87.8 us -> none  [body(): lax.psum(partial_value.astype(jnp.bfloat16), 'tile').astype(jnp.float32)]
    all_gather x0 -> x1, waiting for transfers between devices: none -> 44.5 us  [body(): lax.all_gather(partial_value.astype(jnp.bfloat16), 'tile')]
    reduce_sum x0 -> x1, other arithmetic: none -> 1.88 us  [body(): jnp.sum(lax.all_gather(partial_value.astype(jnp.bfloat16), 'tile'), axis=0)]
where the time goes in v1:
time: 138 us
  waiting for transfers between devices  70.8 us (51%)
  blocking collectives  23.1 us (17%)
  between operations  14.2 us (10%)
  matrix products  10.2 us (7%)
  starting transfers between devices  8.61 us (6%)
  local copies, waits for them, and re-layouts  7.48 us (5%)
  other arithmetic  3.4 us (2%)
    all_gather x1, waiting for transfers between devices, body(): lax.all_gather(partial_value.astype(jnp.bfloat16), 'tile')  44.5 us
    all_to_all x1, waiting for transfers between devices, body(): lax.all_to_all(fields[None], 'freq', split_axis=1, concat_axis=0, tiled=T...  26.3 us
    all_to_all x1, blocking collectives, body(): lax.all_to_all(coeffs, 'tile', split_axis=0, concat_axis=0, tiled=True)  23.1 us
    all_to_all x1, starting transfers between devices, body(): lax.all_to_all(fields[None], 'freq', split_axis=1, concat_axis=0, tiled=T...  8.57 us
    dot_general x1, matrix products, body(): jnp.einsum('irk,rc->ikc', v_factors[0], flat_field, preferred_element_typ...  4.58 us
    unnamed x13, local copies, waits for them, and re-layouts  3.53 us
  transfers between devices with their start and end apart: 2, of which 2 were waited for; matrix products, arithmetic and copies ran while one was open for 1% of the time, Pallas kernels for 0%

profile of v1, /device:TPU:2, one launch (start us, length us, event | category | flops | bytes accessed | tf_op | source)
XLA Modules:
  0.0 137.8 jit_solution(13781497539528874671)
XLA Ops:
  7.2 0.0 copy-start.5
  7.2 1.7 %reshape.180 = bf16[1024,512,1]{1,0,2:T(8,128)(2,1)S(1)} reshape(bf16[1,1024,2,256]{3,2,1,0:T(2,128)(2,1)} %param.8) | data formatting | bytes 2097152 | tf_op jit(solution)/shard_map/reshape;squeeze | solution.py:32
  8.9 0.0 copy-done.5
  8.9 0.0 copy-start.1
  9.0 4.6 %fusion.3 = f32[16,128,512]{2,1,0:T(8,128)S(1)} fusion(bf16[1024,512,1]{1,0,2:T(8,128)(2,1)S(1)} %reshape.180, bf16[1,16,1024,128]{3,2,1,0:T(8,128)(2,1)} %param.9), kind=kOutput, calls=%fused_computation.3 | convolution fusion | flops 2147483648 | bytes 9437184 | tf_op jit(solution)/shard_map/irk,rc->ikc/dot_general | solution.py:33
  13.5 0.0 copy-done.1
  13.6 0.1 fusion.27
  13.6 0.4 fusion.18
  14.0 0.1 pad_maximum_fusion
  14.1 0.1 copy.24
  14.2 23.1 %all_to_all.17 = bf16[16,64,2,256]{3,1,2,0:T(8,128)(2,1)S(1)} all-to-all(bf16[16,64,2,256]{3,1,2,0:T(8,128)(2,1)S(1)} %copy.24), channel_id=1, replica_groups=mesh['freq'=16,'tile'=16] {'tile'}, dimensions={0} | all-to-all | bytes 2097152 | tf_op jit(solution)/shard_map/all_to_all | solution.py:46
  37.3 0.1 slice_bitcast_fusion
  37.4 0.0 copy-start.2
  37.4 0.2 maximum_maximum_fusion
  37.6 1.9 %copy-done.2 = bf16[1,1024,16,128]{3,2,1,0:T(8,128)(2,1)S(1)} copy-done((bf16[1,1024,16,128]{3,2,1,0:T(8,128)(2,1)S(1)}, bf16[1,1024,16,128]{3,2,1,0:T(8,128)(2,1)}, u32[]{:S(2)}) %copy-start.2) | copy-done | bytes 4194328
  39.5 2.4 %fusion.7 = bf16[512,1024]{1,0:T(8,128)(2,1)S(1)} fusion(bf16[2048,512]{1,0:T(8,128)(2,1)S(1)} %bitcast.55, bf16[128,8,16,128]{3,2,1,0:T(8,128)(2,1)S(1)} %bitcast.61), kind=kOutput, calls=%fused_computation.12 | convolution fusion | flops 2148007936 | bytes 7340032 | tf_op jit(solution)/shard_map/dot_general | solution.py:48
  41.9 0.0 copy-start.3
  42.0 0.0 copy-start.4
  42.0 2.0 %copy.26 = bf16[1,1024,2,256]{3,2,0,1:T(2,128)(2,1)} copy(bf16[1,1024,2,256]{1,3,2,0:T(8,128)(2,1)S(1)} %bitcast.58) | data formatting | bytes 2097152 | tf_op jit(solution)/shard_map/convert_element_type | solution.py:51
  44.0 8.6 %all-to-all-start.1 = ((bf16[1,1024,2,256]{3,2,0,1:T(2,128)(2,1)}), bf16[1,1024,2,256]{3,2,0,1:T(2,128)(2,1)S(1)}, u32[]{:S(2)}, u32[]{:S(2)}) async-start(bf16[1,1024,2,256]{3,2,0,1:T(2,128)(2,1)} %copy.26), calls=%async_computation.1 | async-start | bytes 2097152 | tf_op jit(solution)/shard_map/all_to_all | solution.py:53
  52.6 0.0 copy-start
  52.6 0.0 all-gather.3.cloned.1.call-start
  52.7 0.1 multiply_cosine_fusion
  52.8 26.3 %all-to-all-done.1 = bf16[1,1024,2,256]{3,2,0,1:T(2,128)(2,1)S(1)} async-done(((bf16[1,1024,2,256]{3,2,0,1:T(2,128)(2,1)}), bf16[1,1024,2,256]{3,2,0,1:T(2,128)(2,1)S(1)}, u32[]{:S(2)}, u32[]{:S(2)}) %all-to-all-start.1) | async-done | bytes 1048608 | tf_op jit(solution)/shard_map/all_to_all | solution.py:53
  79.1 0.0 copy-done.3
  79.1 1.9 %fusion.5 = bf16[32,64,256]{2,0,1:T(8,128)(2,1)S(1)} fusion(bf16[16,64,2,256]{3,2,1,0:T(2,128)(2,1)S(1)} %bitcast.57, bf16[1,32,64,256]{3,2,1,0:T(8,128)(2,1)S(1)} %copy-done.3, s32[64,256]{1,0:T(8,128)S(1)} %bitcast.62, f32[32,16,1]{0,1,2:T(8,128)S(1)} %get-tuple-element.13, f32[32,16,1]{0,1,2:T(8,128)S(1)} %get-tuple-element.12), kind=kOutput, calls=%fused_computation.7 | convolution fusion | flops 203950080 | bytes 3215360 | tf_op jit(solution)/shard_map/tfc,fscn->tsn/dot_general | solution.py:55
  81.0 1.3 fusion.11
  82.3 0.0 all-gather.3.cloned.1.call-update
  82.3 1.6 %copy.29 = bf16[1,32,64,256]{3,2,1,0:T(8,128)(2,1)} copy(bf16[1,32,64,256]{3,1,2,0:T(8,128)(2,1)S(1)} %bitcast.54) | data formatting | bytes 2097152
  83.9 44.5 %all-gather.3.cloned.1.call-done = bf16[4096,256]{1,0:T(8,128)(2,1)} async-done(((bf16[256,256]{1,0:T(8,128)(2,1)}), bf16[4096,256]{1,0:T(8,128)(2,1)}) %all-gather.3.cloned.1.call-update) | async-done | bytes 2097168 | tf_op jit(solution)/shard_map/all_gather | solution.py:72
  128.4 1.9 %reduce_sum.12 = bf16[256,256]{1,0:T(8,128)(2,1)S(1)} reduce(bf16[16,256,256]{2,1,0:T(8,128)(2,1)} %bitcast.56, bf16[]{:T(256)} %constant.7.clone.1), dimensions={0}, to_apply=%region_0.1 | reduce | flops 983040 | bytes 2228226 | tf_op jit(solution)/shard_map/reduce_sum | solution.py:71
  130.3 0.6 multiply_bitcast_fusion
  (6 shorter events, 0.1 us)
Async XLA Ops:
  7.2 1.8 %copy-start.5 = (s32[1,16,1]{1,2,0:T(1,128)S(1)}, s32[1,16,1]{1,2,0:T(1,128)}, u32[]{:S(2)}) copy-start(s32[1,16,1]{1,2,0:T(1,128)} %param.12) | copy-start | bytes 196
  8.9 4.6 %copy-start.1 = (s32[1,16,1]{1,2,0:T(1,128)S(1)}, s32[1,16,1]{1,2,0:T(1,128)}, u32[]{:S(2)}) copy-start(s32[1,16,1]{1,2,0:T(1,128)} %param.11) | copy-start | bytes 196
  37.4 2.2 %copy-start.2 = (bf16[1,1024,16,128]{3,2,1,0:T(8,128)(2,1)S(1)}, bf16[1,1024,16,128]{3,2,1,0:T(8,128)(2,1)}, u32[]{:S(2)}) copy-start(bf16[1,1024,16,128]{3,2,1,0:T(8,128)(2,1)} %param.10) | copy-start | bytes 12582916
  41.9 37.1 %copy-start.3 = (bf16[1,32,64,256]{3,2,1,0:T(8,128)(2,1)S(1)}, bf16[1,32,64,256]{3,2,1,0:T(8,128)(2,1)}, u32[]{:S(2)}) copy-start(bf16[1,32,64,256]{3,2,1,0:T(8,128)(2,1)} %param.13) | copy-start | bytes 3145732
  42.0 37.1 %copy-start.4 = (s32[1,64,256]{2,1,0:T(8,128)S(1)}, s32[1,64,256]{2,1,0:T(8,128)}, u32[]{:S(2)}) copy-start(s32[1,64,256]{2,1,0:T(8,128)} %param.14) | copy-start | bytes 196612
  44.0 35.1 %all-to-all-start.1 = ((bf16[1,1024,2,256]{3,2,0,1:T(2,128)(2,1)}), bf16[1,1024,2,256]{3,2,0,1:T(2,128)(2,1)S(1)}, u32[]{:S(2)}, u32[]{:S(2)}) async-start(bf16[1,1024,2,256]{3,2,0,1:T(2,128)(2,1)} %copy.26), calls=%async_computation.1 | async-start | bytes 2097152 | tf_op jit(solution)/shard_map/all_to_all | solution.py:53
  52.6 28.4 %copy-start = (f32[1,64]{1,0:T(1,128)S(1)}, f32[1,64]{1,0:T(1,128)}, u32[]{:S(2)}) copy-start(f32[1,64]{1,0:T(1,128)} %param.15) | copy-start | bytes 772
  52.6 75.9 %all-gather.3.cloned.1.call-start = ((), (), s32[]{:S(2)}) async-start(), calls=%async_computation.2 | async-start | bytes 2228224 | tf_op jit(solution)/shard_map/all_gather | solution.py:72
Sparse Core Ops, SparseCore 0:
  82.5 45.9 all-gather.2
